TPU v7x, 256 devices: a whole 4x4x8 slice. The times are simulated.
256 devices in a mesh: feat: 32 (over y, z), dp: 8 (over x, core).
Axes of the slice: x: 4, y: 4, z: 8, core: 2. Of those that a mesh axis runs over, the one named last changes fastest.
Arguments:
- face_grid: bfloat16 [32768, 10240], P('dp', 'feat'), may hold values from -6 to 6
- first_nbrs: int32 [16384, 8], P('dp'), may hold values from 0 to 4095
- first_count: int32 [16384], P('dp'), may hold values from 1 to 8
- w_first: bfloat16 [10240, 256], P('feat'), may hold values from -0.0625 to 0.0625
- b_first: float32 [256], replicated, may hold values from -3 to 3
- send_rows: int32 [4096], P('dp'), may hold values from 0 to 2047
- second_nbrs: int32 [16384, 8], P(('dp', 'feat')), may hold values from 0 to 2559
- second_count: int32 [16384], P(('dp', 'feat')), may hold values from 1 to 8
- w_in: bfloat16 [256, 1024], replicated, may hold values from -0.375 to 0.375
- w_out: bfloat16 [1024, 256], replicated, may hold values from -0.1875 to 0.1875
- out_grad: bfloat16 [16384, 256], P(('dp', 'feat')), may hold values from -6 to 6
Outputs:
- embed: bfloat16 [16384, 256], P(('dp', 'feat'))
- grad_first: float32 [10240, 256], P('feat')
Inputs may be any that keep to these rules, and one draw needn't show every extreme that they name: `first_count`: slots at or past a target's count are ignored; counts lie in 1 to 8. `first_nbrs`: only slots below first_count are read. `second_count`: slots at or past a target's count are ignored. `second_nbrs`: indices below 2048 name the partition's own targets, the rest the faces received from the previous partition in order; only slots below second_count are read. `send_rows`: entries may repeat.
All inputs are finite; a program needn't handle non-finite values.
Results may differ from a plain program's by a relative error of at most 0.0061.
Values may be sent and summed in bfloat16 or wider, within the bound.
No kernel may reach another device: no remote copies, remote signals or barrier semaphores. Data moves between devices by JAX's collectives and lax.ppermute only.
A program may use at most 64 MiB of HBM per device.

v0:
```python
import jax
import jax.numpy as jnp
from jax import lax
from jax.sharding import PartitionSpec as P


def passed_along(shard, axis, by):
    devices = lax.axis_size(axis)
    return lax.ppermute(shard, axis, [(i, (i + by) % devices) for i in range(devices)])


def slope(value):
    sig = jax.nn.sigmoid(value)
    return sig * (1.0 + value * (1.0 - sig))


def mean_rows(table, nbrs, count):
    total = jnp.zeros((nbrs.shape[0], table.shape[1]), jnp.float32)
    for slot in range(nbrs.shape[1]):
        picked = table[nbrs[:, slot]].astype(jnp.float32)
        total = total + jnp.where((slot < count)[:, None], picked, 0.0)
    return total / count[:, None].astype(jnp.float32)


def spread(grad, nbrs, count, size):
    slots = jnp.arange(nbrs.shape[1], dtype=jnp.int32)
    factor = jnp.where(
        slots[None, :] < count[:, None], 1.0 / count[:, None].astype(jnp.float32), 0.0
    )
    terms = (grad[:, None, :] * factor[:, :, None]).reshape(-1, grad.shape[1])
    return jax.ops.segment_sum(terms, nbrs.reshape(-1), num_segments=size)


def body(
    face_grid,
    first_nbrs,
    first_count,
    w_first,
    b_first,
    send_rows,
    second_nbrs,
    second_count,
    w_in,
    w_out,
    out_grad,
):
    targets = first_nbrs.shape[0]
    agg_first = (
        face_grid[:targets].astype(jnp.float32) + mean_rows(face_grid, first_nbrs, first_count)
    ).astype(jnp.bfloat16)
    partial_value = jnp.dot(agg_first, w_first, preferred_element_type=jnp.float32)
    pre_own = lax.psum_scatter(partial_value, "feat", scatter_dimension=0, tiled=True) + b_first
    hidden_own = jax.nn.silu(pre_own).astype(jnp.bfloat16)
    table = lax.all_gather(hidden_own, "feat", axis=0, tiled=True)
    received = passed_along(table[send_rows], "dp", 1)
    extended = jnp.concatenate([table, received], axis=0)
    agg_second = (
        hidden_own.astype(jnp.float32) + mean_rows(extended, second_nbrs, second_count)
    ).astype(jnp.bfloat16)
    pre_mlp = jnp.dot(agg_second, w_in, preferred_element_type=jnp.float32)
    act_mlp = jax.nn.silu(pre_mlp).astype(jnp.bfloat16)
    embed = (
        hidden_own.astype(jnp.float32) + jnp.dot(act_mlp, w_out, preferred_element_type=jnp.float32)
    ).astype(jnp.bfloat16)
    grad_act = lax.dot_general(
        out_grad, w_out, (((1,), (1,)), ((), ())), preferred_element_type=jnp.float32
    )
    grad_pre_mlp = (grad_act * slope(pre_mlp)).astype(jnp.bfloat16)
    grad_agg = lax.dot_general(
        grad_pre_mlp, w_in, (((1,), (1,)), ((), ())), preferred_element_type=jnp.float32
    )
    grad_ext = spread(grad_agg, second_nbrs, second_count, extended.shape[0])
    full_rows = table.shape[0]
    returned = passed_along(grad_ext[full_rows:].astype(jnp.bfloat16), "dp", -1).astype(jnp.float32)
    table_grad = grad_ext[:full_rows].at[send_rows].add(returned)
    own_terms = out_grad.astype(jnp.float32) + grad_agg
    grad_own = (
        lax.psum_scatter(
            table_grad.astype(jnp.bfloat16), "feat", scatter_dimension=0, tiled=True
        ).astype(jnp.float32)
        + own_terms
    )
    grad_pre_own = (grad_own * slope(pre_own)).astype(jnp.bfloat16)
    grad_pre_first = lax.all_gather(grad_pre_own, "feat", axis=0, tiled=True)
    slice_grad = lax.dot_general(
        agg_first, grad_pre_first, (((0,), (0,)), ((), ())), preferred_element_type=jnp.float32
    )
    grad_first = lax.psum(slice_grad, "dp")
    return (embed, grad_first)


def solution(mesh):
    return jax.shard_map(
        body,
        mesh=mesh,
        in_specs=(
            P("dp", "feat"),
            P("dp", None),
            P("dp"),
            P("feat", None),
            P(),
            P("dp"),
            P(("dp", "feat"), None),
            P(("dp", "feat")),
            P(),
            P(),
            P(("dp", "feat"), None),
        ),
        out_specs=(P(("dp", "feat"), None), P("feat", None)),
        check_vma=False,
    )
```

profile of v0, /device:TPU:8, one launch (start us, length us, event | category | flops | bytes accessed | tf_op | source)
XLA Modules:
  0.0 828.4 jit_solution(5859287706951482798)
XLA Ops:
  7.2 0.0 copy-start
  7.2 0.0 reduce-scatter.3.cloned.1.call-start
  7.2 0.8 broadcast_compare_fusion.7
  8.0 0.7 convert_element_type.107
  8.7 4.6 copy.22
  13.3 0.0 copy-done.5
  13.3 0.1 compare_select_fusion.7
  13.4 11.2 %gather_fusion = bf16[2048,320]{1,0:T(8,128)(2,1)} fusion(bf16[4096,320]{1,0:T(8,128)(2,1)} %copy.22, s32[2048]{0:T(1024)S(1)} %broadcast_clamp_fusion.7), kind=kCustom, calls=%fused_computation | custom fusion | bytes 2629632 | tf_op jit(solution)/shard_map/gather | solution.py:20
  24.6 11.2 %gather_fusion.1 = bf16[2048,320]{1,0:T(8,128)(2,1)} fusion(bf16[4096,320]{1,0:T(8,128)(2,1)} %copy.22, s32[2048]{0:T(1024)S(1)} %broadcast_clamp_fusion.6), kind=kCustom, calls=%fused_computation.1 | custom fusion | bytes 2629632 | tf_op jit(solution)/shard_map/gather | solution.py:20
  35.8 11.2 %gather_fusion.2 = bf16[2048,320]{1,0:T(8,128)(2,1)} fusion(bf16[4096,320]{1,0:T(8,128)(2,1)} %copy.22, s32[2048]{0:T(1024)S(1)} %broadcast_clamp_fusion.5), kind=kCustom, calls=%fused_computation.2 | custom fusion | bytes 2629632 | tf_op jit(solution)/shard_map/gather | solution.py:20
  47.0 11.2 %gather_fusion.3 = bf16[2048,320]{1,0:T(8,128)(2,1)} fusion(bf16[4096,320]{1,0:T(8,128)(2,1)} %copy.22, s32[2048]{0:T(1024)S(1)} %broadcast_clamp_fusion.4), kind=kCustom, calls=%fused_computation.3 | custom fusion | bytes 2629632 | tf_op jit(solution)/shard_map/gather | solution.py:20
  58.1 11.2 %gather_fusion.4 = bf16[2048,320]{1,0:T(8,128)(2,1)} fusion(bf16[4096,320]{1,0:T(8,128)(2,1)} %copy.22, s32[2048]{0:T(1024)S(1)} %broadcast_clamp_fusion.3), kind=kCustom, calls=%fused_computation.4 | custom fusion | bytes 2629632 | tf_op jit(solution)/shard_map/gather | solution.py:20
  69.3 11.2 %gather_fusion.5 = bf16[2048,320]{1,0:T(8,128)(2,1)} fusion(bf16[4096,320]{1,0:T(8,128)(2,1)} %copy.22, s32[2048]{0:T(1024)S(1)} %broadcast_clamp_fusion.2), kind=kCustom, calls=%fused_computation.5 | custom fusion | bytes 2629632 | tf_op jit(solution)/shard_map/gather | solution.py:20
  80.5 11.2 %gather_fusion.6 = bf16[2048,320]{1,0:T(8,128)(2,1)} fusion(bf16[4096,320]{1,0:T(8,128)(2,1)} %copy.22, s32[2048]{0:T(1024)S(1)} %broadcast_clamp_fusion.1), kind=kCustom, calls=%fused_computation.6 | custom fusion | bytes 2629632 | tf_op jit(solution)/shard_map/gather | solution.py:20
  91.7 11.2 %gather_fusion.7 = bf16[2048,320]{1,0:T(8,128)(2,1)} fusion(bf16[4096,320]{1,0:T(8,128)(2,1)} %copy.22, s32[2048]{0:T(1024)S(1)} %broadcast_clamp_fusion), kind=kCustom, calls=%fused_computation.7 | custom fusion | bytes 2629632 | tf_op jit(solution)/shard_map/gather | solution.py:20
  102.8 8.9 %add_convert_fusion = bf16[2048,320]{1,0:T(8,128)(2,1)S(1)} fusion(bf16[2048,320]{1,0:T(8,128)(2,1)} %gather_fusion.7, bf16[2048,320]{1,0:T(8,128)(2,1)} %gather_fusion.6, bf16[2048,320]{1,0:T(8,128)(2,1)} %gather_fusion.5, bf16[2048,320]{1,0:T(8,128)(2,1)} %gather_fusion.4, bf16[2048,320]{1,0:T(8,128)(2,1)} %gather_fusion.3, ...), kind=kLoop, calls=%fused_computation.19 | loop fusion | flops 17694720 | bytes 13131776 | tf_op jit(solution)/shard_map/convert_element_type | solution.py:50
  111.8 2.0 fusion.40
  113.8 0.0 reduce-scatter.3.cloned.1.call-update
  113.8 0.0 all-gather.3.cloned.1.call-start
  113.9 220.8 %reduce-scatter.3.cloned.1.call-done = f32[64,256]{1,0:T(8,128)} async-done(((f32[2048,256]{1,0:T(8,128)}), f32[64,256]{1,0:T(8,128)}) %reduce-scatter.3.cloned.1.call-update) | async-done | bytes 65552 | tf_op jit(solution)/shard_map/reduce_scatter | solution.py:52
  334.7 1.5 multiply_convert_fusion.3
  336.2 0.0 all-gather.3.cloned.1.call-update
  336.2 0.2 reduce-scatter.5.cloned.1.call-start
  336.6 0.1 fusion.28
  336.6 75.6 %all-gather.3.cloned.1.call-done = bf16[2048,256]{1,0:T(8,128)(2,1)} async-done(((bf16[64,256]{1,0:T(8,128)(2,1)}), bf16[2048,256]{1,0:T(8,128)(2,1)}) %all-gather.3.cloned.1.call-update) | async-done | bytes 1048592 | tf_op jit(solution)/shard_map/all_gather | solution.py:54
  412.2 3.6 gather_fusion.8
  415.9 0.0 collective-permute-start
  415.9 0.1 copy.31
  416.0 0.1 select_n.163
  416.1 0.1 reshape.203
  416.2 1.1 constant_dynamic-update-slice_fusion.1
  417.3 5.8 collective-permute-done
  423.1 0.7 constant_dynamic-update-slice_fusion
  423.8 2.1 gather_fusion.10
  426.0 0.0 copy-start.6
  426.0 0.0 copy-start.11
  426.0 2.2 gather_fusion.11
  428.2 2.1 gather_fusion.12
  430.3 2.1 gather_fusion.13
  432.5 2.1 gather_fusion.14
  434.6 2.1 gather_fusion.15
  436.8 2.1 gather_fusion.9
  438.9 2.1 gather_fusion.16
  441.1 0.3 fusion.16
  441.4 0.5 fusion.3
  441.9 5.1 scatter_custom_fusion
  447.0 1.1 slice.132
  448.0 0.0 collective-permute-start.1
  448.1 3.1 slice.112
  451.2 0.8 collective-permute-done.1
  451.9 6.0 scatter_custom_fusion.1
  457.9 2.7 convert_element_type.125
  460.6 0.0 reduce-scatter.5.cloned.1.call-update
  460.7 0.0 all-gather.5.cloned.1.call-start
  460.7 215.0 %reduce-scatter.5.cloned.1.call-done = bf16[64,256]{1,0:T(8,128)(2,1)} async-done(((bf16[2048,256]{1,0:T(8,128)(2,1)}), bf16[64,256]{1,0:T(8,128)(2,1)}) %reduce-scatter.5.cloned.1.call-update) | async-done | bytes 32784 | tf_op jit(solution)/shard_map/reduce_scatter | solution.py:78
  675.8 1.4 multiply_convert_fusion.2
  677.2 0.0 all-gather.5.cloned.1.call-update
  677.2 0.0 all-reduce.2.cloned.1.call-start
  677.2 75.9 %all-gather.5.cloned.1.call-done = bf16[2048,256]{1,0:T(8,128)(2,1)} async-done(((bf16[64,256]{1,0:T(8,128)(2,1)}), bf16[2048,256]{1,0:T(8,128)(2,1)}) %all-gather.5.cloned.1.call-update) | async-done | bytes 1048592 | tf_op jit(solution)/shard_map/all_gather | solution.py:84
  753.1 2.5 fusion.41
  755.7 0.0 all-reduce.2.cloned.1.call-update
  755.7 0.8 fusion.4
  756.6 63.6 %all-reduce.2.cloned.1.call-done = f32[320,256]{1,0:T(8,128)} async-done(((f32[320,256]{1,0:T(8,128)}), f32[320,256]{1,0:T(8,128)}) %all-reduce.2.cloned.1.call-update) | async-done | bytes 327696 | tf_op jit(solution)/shard_map/psum | solution.py:88
  820.1 1.7 copy.35
  (38 shorter events, 0.1 us)
Async XLA Ops:
  7.2 433.9 %copy-start = (bf16[256,1024]{1,0:T(8,128)(2,1)S(1)}, bf16[256,1024]{1,0:T(8,128)(2,1)}, u32[]{:S(2)}) copy-start(bf16[256,1024]{1,0:T(8,128)(2,1)} %param.19) | copy-start | bytes 1572868
  7.2 327.5 %reduce-scatter.3.cloned.1.call-start = ((), (), s32[]{:S(2)}) async-start(), calls=%async_computation.2 | async-start | bytes 2162688 | tf_op jit(solution)/shard_map/reduce_scatter | solution.py:52
  8.7 4.6 copy-start.5
  102.8 8.9 %copy-start.3 = (bf16[320,256]{1,0:T(8,128)(2,1)S(1)}, bf16[320,256]{1,0:T(8,128)(2,1)}, u32[]{:S(2)}) copy-start(bf16[320,256]{1,0:T(8,128)(2,1)} %param.14) | copy-start | bytes 491524
  113.8 220.9 %copy-start.8 = (f32[256]{0:T(256)S(1)}, f32[256]{0:T(256)}, u32[]{:S(2)}) copy-start(f32[256]{0:T(256)} %param.15) | copy-start | bytes 3076
  113.8 222.6 %copy-start.10 = (s32[512]{0:T(512)S(1)}, s32[512]{0:T(512)}, u32[]{:S(2)}) copy-start(s32[512]{0:T(512)} %param.16) | copy-start | bytes 6148
  113.8 222.7 %copy-start.7 = (s32[64,8]{0,1:T(8,128)S(1)}, s32[64,8]{0,1:T(8,128)}, u32[]{:S(2)}) copy-start(s32[64,8]{0,1:T(8,128)} %param.17) | copy-start | bytes 6148
  113.8 222.7 %copy-start.9 = (s32[64]{0:T(128)S(1)}, s32[64]{0:T(128)}, u32[]{:S(2)}) copy-start(s32[64]{0:T(128)} %param.18) | copy-start | bytes 772
  113.8 298.4 %all-gather.3.cloned.1.call-start = ((), (), s32[]{:S(2)}) async-start(), calls=%async_computation.3 | async-start | bytes 1081344 | tf_op jit(solution)/shard_map/all_gather | solution.py:54
  336.2 339.6 %reduce-scatter.5.cloned.1.call-start = ((), (), s32[]{:S(2)}) async-start(), calls=%async_computation.4 | async-start | bytes 1081344 | tf_op jit(solution)/shard_map/reduce_scatter | solution.py:78
  412.2 3.9 copy-start.1
  415.9 7.2 collective-permute-start
  417.3 23.8 %copy-start.4 = (bf16[64,256]{1,0:T(8,128)(2,1)S(1)}, bf16[64,256]{1,0:T(8,128)(2,1)}, u32[]{:S(2)}) copy-start(bf16[64,256]{1,0:T(8,128)(2,1)} %multiply_convert_fusion.3) | copy-start | bytes 98308
  426.0 15.4 %copy-start.6 = (bf16[64,256]{1,0:T(8,128)(2,1)S(1)}, bf16[64,256]{1,0:T(8,128)(2,1)}, u32[]{:S(2)}) copy-start(bf16[64,256]{1,0:T(8,128)(2,1)} %param.21) | copy-start | bytes 98308
  426.0 15.4 %copy-start.11 = (bf16[1024,256]{1,0:T(8,128)(2,1)S(1)}, bf16[1024,256]{1,0:T(8,128)(2,1)}, u32[]{:S(2)}) copy-start(bf16[1024,256]{1,0:T(8,128)(2,1)} %param.20) | copy-start | bytes 1572868
  448.0 3.9 collective-permute-start.1
  457.9 217.8 %copy-start.2 = (f32[64,256]{1,0:T(8,128)S(1)}, f32[64,256]{1,0:T(8,128)}, u32[]{:S(2)}) copy-start(f32[64,256]{1,0:T(8,128)} %reduce-scatter.3.cloned.1.call-done) | copy-start | bytes 196612
  460.7 292.5 %all-gather.5.cloned.1.call-start = ((), (), s32[]{:S(2)}) async-start(), calls=%async_computation.5 | async-start | bytes 1081344 | tf_op jit(solution)/shard_map/all_gather | solution.py:84
  677.2 142.9 %all-reduce.2.cloned.1.call-start = ((), (), s32[]{:S(2)}) async-start(), calls=%async_computation.6 | async-start | bytes 655360 | tf_op jit(solution)/shard_map/psum | solution.py:88
Sparse Core Ops, SparseCore 0:
  113.9 220.6 reduce-scatter.2
  337.8 74.3 all-gather.2
  460.8 214.9 reduce-scatter.4
  678.8 74.3 all-gather.4
  755.9 64.2 all-reduce.1
where the time goes:
time: 830 us; the launch traced here: 828 us
  waiting for transfers between devices  658 us (79%)
  local copies, waits for them, and re-layouts  123 us (15%)
  other arithmetic  27.3 us (3%)
  between operations  14 us (2%)
    reduce_scatter x1, waiting for transfers between devices, body(): lax.psum_scatter(partial_value, 'feat', scatter_dimension=0, tiled=True)  221 us
    reduce_scatter x1, waiting for transfers between devices, body(): lax.psum_scatter(table_grad.astype(jnp.bfloat16), 'feat', scatter_dimensi...  215 us
    gather x16, local copies, waits for them, and re-layouts, mean_rows(): picked = table[nbrs[:, slot]].astype(jnp.float32)  107 us
    all_gather x1, waiting for transfers between devices, body(): grad_pre_first = lax.all_gather(grad_pre_own, 'feat', axis=0, tiled=True)  75.9 us
    all_gather x1, waiting for transfers between devices, body(): table = lax.all_gather(hidden_own, 'feat', axis=0, tiled=True)  75.6 us
    psum x1, waiting for transfers between devices, body(): grad_first = lax.psum(slice_grad, 'dp')  63.6 us
  transfers between devices with their start and end apart: 7, of which 7 were waited for; matrix products, arithmetic and copies ran while one was open for 1% of the time, Pallas kernels for 0%

commit v1 on v0

--- a/solution.py
+++ b/solution.py
@@ -1,7 +1,19 @@
+import functools
 import jax
 import jax.numpy as jnp
 from jax import lax
 from jax.sharding import PartitionSpec as P
+from jax.lax import all_to_all, psum
+
+
+def solve_tiles(s0, dimension_no):
+    earlier = psum(1, "feat")
+    base_arr = jnp.stack(earlier * [s0], axis=0)
+    upper = all_to_all(base_arr, "feat", concat_axis=0, split_axis=0)
+    return jnp.concatenate(upper, axis=dimension_no)
+
+
+update_numbers = functools.partial(solve_tiles, dimension_no=0)
 
 
 def passed_along(shard, axis, by):
@@ -51,7 +63,7 @@
     partial_value = jnp.dot(agg_first, w_first, preferred_element_type=jnp.float32)
     pre_own = lax.psum_scatter(partial_value, "feat", scatter_dimension=0, tiled=True) + b_first
     hidden_own = jax.nn.silu(pre_own).astype(jnp.bfloat16)
-    table = lax.all_gather(hidden_own, "feat", axis=0, tiled=True)
+    table = update_numbers(hidden_own)
     received = passed_along(table[send_rows], "dp", 1)
     extended = jnp.concatenate([table, received], axis=0)
     agg_second = (

time: 830 us -> 784 us (0.945)
  waiting for transfers between devices: 658 us -> 600 us
    all_gather x1 -> x0, waiting for transfers between devices: 75.6 us -> none  [body(): table = lax.all_gather(hidden_own, 'feat', axis=0, tiled=True)]
    all_to_all x0 -> x1, waiting for transfers between devices: none -> 19.3 us  [solve_tiles(): upper = all_to_all(base_arr, 'feat', concat_axis=0, split_axis=0)]
where the time goes in v1:
time: 784 us; the launch traced here: 783 us
  waiting for transfers between devices  600 us (77%)
  local copies, waits for them, and re-layouts  121 us (15%)
  other arithmetic  30.9 us (4%)
  between operations  14 us (2%)
  starting transfers between devices  8.4 us (1%)
  matrix products  8.15 us (1%)
    reduce_scatter x1, waiting for transfers between devices, body(): lax.psum_scatter(partial_value, 'feat', scatter_dimension=0, tiled=True)  221 us
    reduce_scatter x1, waiting for transfers between devices, body(): lax.psum_scatter(table_grad.astype(jnp.bfloat16), 'feat', scatter_dimensi...  215 us
    gather x16, local copies, waits for them, and re-layouts, mean_rows(): picked = table[nbrs[:, slot]].astype(jnp.float32)  106 us
    all_gather x1, waiting for transfers between devices, body(): grad_pre_first = lax.all_gather(grad_pre_own, 'feat', axis=0, tiled=True)  76.1 us
    psum x1, waiting for transfers between devices, body(): grad_first = lax.psum(slice_grad, 'dp')  63.6 us
    all_to_all x1, waiting for transfers between devices, solve_tiles(): upper = all_to_all(base_arr, 'feat', concat_axis=0, split_axis=0)  19.3 us
  transfers between devices with their start and end apart: 7, of which 7 were waited for; matrix products, arithmetic and copies ran while one was open for 1% of the time, Pallas kernels for 0%

profile of v1, /device:TPU:8, one launch (start us, length us, event | category | flops | bytes accessed | tf_op | source)
XLA Modules:
  0.0 783.0 jit_solution(17550370614504803622)
XLA Ops:
  7.2 0.0 copy-start
  7.2 0.0 reduce-scatter.3.cloned.1.call-start
  7.2 0.8 broadcast_compare_fusion.7
  8.0 0.7 convert_element_type.107
  8.7 4.6 copy.22
  13.3 0.1 compare_select_fusion.7
  13.4 11.2 %gather_fusion = bf16[2048,320]{1,0:T(8,128)(2,1)} fusion(bf16[4096,320]{1,0:T(8,128)(2,1)} %copy.22, s32[2048]{0:T(1024)S(1)} %broadcast_clamp_fusion.7), kind=kCustom, calls=%fused_computation | custom fusion | bytes 2629632 | tf_op jit(solution)/shard_map/gather | solution.py:32
  24.5 11.2 %gather_fusion.1 = bf16[2048,320]{1,0:T(8,128)(2,1)} fusion(bf16[4096,320]{1,0:T(8,128)(2,1)} %copy.22, s32[2048]{0:T(1024)S(1)} %broadcast_clamp_fusion.6), kind=kCustom, calls=%fused_computation.1 | custom fusion | bytes 2629632 | tf_op jit(solution)/shard_map/gather | solution.py:32
  35.7 11.1 %gather_fusion.2 = bf16[2048,320]{1,0:T(8,128)(2,1)} fusion(bf16[4096,320]{1,0:T(8,128)(2,1)} %copy.22, s32[2048]{0:T(1024)S(1)} %broadcast_clamp_fusion.5), kind=kCustom, calls=%fused_computation.2 | custom fusion | bytes 2629632 | tf_op jit(solution)/shard_map/gather | solution.py:32
  46.8 11.1 %gather_fusion.3 = bf16[2048,320]{1,0:T(8,128)(2,1)} fusion(bf16[4096,320]{1,0:T(8,128)(2,1)} %copy.22, s32[2048]{0:T(1024)S(1)} %broadcast_clamp_fusion.4), kind=kCustom, calls=%fused_computation.3 | custom fusion | bytes 2629632 | tf_op jit(solution)/shard_map/gather | solution.py:32
  58.0 11.1 %gather_fusion.4 = bf16[2048,320]{1,0:T(8,128)(2,1)} fusion(bf16[4096,320]{1,0:T(8,128)(2,1)} %copy.22, s32[2048]{0:T(1024)S(1)} %broadcast_clamp_fusion.3), kind=kCustom, calls=%fused_computation.4 | custom fusion | bytes 2629632 | tf_op jit(solution)/shard_map/gather | solution.py:32
  69.1 11.2 %gather_fusion.5 = bf16[2048,320]{1,0:T(8,128)(2,1)} fusion(bf16[4096,320]{1,0:T(8,128)(2,1)} %copy.22, s32[2048]{0:T(1024)S(1)} %broadcast_clamp_fusion.2), kind=kCustom, calls=%fused_computation.5 | custom fusion | bytes 2629632 | tf_op jit(solution)/shard_map/gather | solution.py:32
  80.3 11.2 %gather_fusion.6 = bf16[2048,320]{1,0:T(8,128)(2,1)} fusion(bf16[4096,320]{1,0:T(8,128)(2,1)} %copy.22, s32[2048]{0:T(1024)S(1)} %broadcast_clamp_fusion.1), kind=kCustom, calls=%fused_computation.6 | custom fusion | bytes 2629632 | tf_op jit(solution)/shard_map/gather | solution.py:32
  91.4 11.2 %gather_fusion.7 = bf16[2048,320]{1,0:T(8,128)(2,1)} fusion(bf16[4096,320]{1,0:T(8,128)(2,1)} %copy.22, s32[2048]{0:T(1024)S(1)} %broadcast_clamp_fusion), kind=kCustom, calls=%fused_computation.7 | custom fusion | bytes 2629632 | tf_op jit(solution)/shard_map/gather | solution.py:32
  102.6 8.9 %add_convert_fusion = bf16[2048,320]{1,0:T(8,128)(2,1)S(1)} fusion(bf16[2048,320]{1,0:T(8,128)(2,1)} %gather_fusion.7, bf16[2048,320]{1,0:T(8,128)(2,1)} %gather_fusion.6, bf16[2048,320]{1,0:T(8,128)(2,1)} %gather_fusion.5, bf16[2048,320]{1,0:T(8,128)(2,1)} %gather_fusion.4, bf16[2048,320]{1,0:T(8,128)(2,1)} %gather_fusion.3, ...), kind=kLoop, calls=%fused_computation.19 | loop fusion | flops 17694720 | bytes 13131776 | tf_op jit(solution)/shard_map/convert_element_type | solution.py:62
  111.5 2.0 fusion.40
  113.5 0.0 reduce-scatter.3.cloned.1.call-update
  113.6 220.8 %reduce-scatter.3.cloned.1.call-done = f32[64,256]{1,0:T(8,128)} async-done(((f32[2048,256]{1,0:T(8,128)}), f32[64,256]{1,0:T(8,128)}) %reduce-scatter.3.cloned.1.call-update) | async-done | bytes 65552 | tf_op jit(solution)/shard_map/reduce_scatter | solution.py:64
  334.4 0.9 multiply_convert_fusion.3
  335.3 1.1 stack.2
  336.4 8.0 %all-to-all-start = ((bf16[32,64,256]{2,1,0:T(8,128)(2,1)}), bf16[32,64,256]{2,1,0:T(8,128)(2,1)S(1)}, u32[]{:S(2)}, u32[]{:S(2)}) async-start(bf16[32,64,256]{2,1,0:T(8,128)(2,1)} %stack.2), calls=%async_computation.1 | async-start | bytes 2097152 | tf_op jit(solution)/shard_map/all_to_all | solution.py:12
  344.5 0.2 reduce-scatter.5.cloned.1.call-start
  344.8 0.6 pad_clamp_fusion.4
  345.3 0.6 pad_clamp_fusion.2
  346.0 0.1 fusion.28
  346.0 19.3 %all-to-all-done = bf16[32,64,256]{2,1,0:T(8,128)(2,1)S(1)} async-done(((bf16[32,64,256]{2,1,0:T(8,128)(2,1)}), bf16[32,64,256]{2,1,0:T(8,128)(2,1)S(1)}, u32[]{:S(2)}, u32[]{:S(2)}) %all-to-all-start) | async-done | bytes 1048608 | tf_op jit(solution)/shard_map/all_to_all | solution.py:12
  365.3 2.6 gather_fusion.8
  367.9 0.6 pad_clamp_fusion
  368.5 0.6 convert_element_type.119
  369.1 0.1 copy.31
  369.2 0.1 select_n.163
  369.3 0.7 reshape.209
  369.9 0.6 broadcast_compare_fusion.15
  370.5 4.5 collective-permute-done
  375.1 1.2 pad_maximum_fusion
  376.3 2.2 gather_fusion.10
  378.5 2.3 gather_fusion.11
  380.8 2.7 gather_fusion.12
  383.5 2.9 gather_fusion.13
  386.4 2.9 gather_fusion.14
  389.3 1.4 gather_fusion.15
  390.7 1.3 gather_fusion.9
  392.0 1.4 gather_fusion.16
  393.4 1.2 fusion.16
  394.6 1.6 fusion.3
  396.2 5.2 scatter_custom_fusion
  401.4 1.1 slice.132
  402.4 0.0 collective-permute-start.1
  402.5 3.1 slice.112
  405.5 0.8 collective-permute-done.1
  406.3 6.0 scatter_custom_fusion.1
  412.3 2.7 convert_element_type.125
  415.0 0.0 reduce-scatter.5.cloned.1.call-update
  415.0 0.0 all-gather.2.cloned.1.call-start
  415.1 215.0 %reduce-scatter.5.cloned.1.call-done = bf16[64,256]{1,0:T(8,128)(2,1)} async-done(((bf16[2048,256]{1,0:T(8,128)(2,1)}), bf16[64,256]{1,0:T(8,128)(2,1)}) %reduce-scatter.5.cloned.1.call-update) | async-done | bytes 32784 | tf_op jit(solution)/shard_map/reduce_scatter | solution.py:90
  630.1 1.4 multiply_convert_fusion.2
  631.5 0.0 all-gather.2.cloned.1.call-update
  631.6 0.0 all-reduce.2.cloned.1.call-start
  631.6 76.1 %all-gather.2.cloned.1.call-done = bf16[2048,256]{1,0:T(8,128)(2,1)} async-done(((bf16[64,256]{1,0:T(8,128)(2,1)}), bf16[2048,256]{1,0:T(8,128)(2,1)}) %all-gather.2.cloned.1.call-update) | async-done | bytes 1048592 | tf_op jit(solution)/shard_map/all_gather | solution.py:96
  707.7 2.5 fusion.41
  710.3 0.0 all-reduce.2.cloned.1.call-update
  710.3 0.8 fusion.4
  711.1 63.6 %all-reduce.2.cloned.1.call-done = f32[320,256]{1,0:T(8,128)} async-done(((f32[320,256]{1,0:T(8,128)}), f32[320,256]{1,0:T(8,128)}) %all-reduce.2.cloned.1.call-update) | async-done | bytes 327696 | tf_op jit(solution)/shard_map/psum | solution.py:100
  774.7 1.7 copy.34
  (37 shorter events, 0.1 us)
Async XLA Ops:
  7.2 386.3 %copy-start = (bf16[256,1024]{1,0:T(8,128)(2,1)S(1)}, bf16[256,1024]{1,0:T(8,128)(2,1)}, u32[]{:S(2)}) copy-start(bf16[256,1024]{1,0:T(8,128)(2,1)} %param.19) | copy-start | bytes 1572868
  7.2 327.2 %reduce-scatter.3.cloned.1.call-start = ((), (), s32[]{:S(2)}) async-start(), calls=%async_computation.3 | async-start | bytes 2162688 | tf_op jit(solution)/shard_map/reduce_scatter | solution.py:64
  8.7 4.6 copy-start.4
  102.6 8.9 %copy-start.3 = (bf16[320,256]{1,0:T(8,128)(2,1)S(1)}, bf16[320,256]{1,0:T(8,128)(2,1)}, u32[]{:S(2)}) copy-start(bf16[320,256]{1,0:T(8,128)(2,1)} %param.14) | copy-start | bytes 491524
  113.5 220.9 %copy-start.7 = (f32[256]{0:T(256)S(1)}, f32[256]{0:T(256)}, u32[]{:S(2)}) copy-start(f32[256]{0:T(256)} %param.15) | copy-start | bytes 3076
  335.3 9.4 %copy-start.10 = (s32[512]{0:T(512)S(1)}, s32[512]{0:T(512)}, u32[]{:S(2)}) copy-start(s32[512]{0:T(512)} %param.16) | copy-start | bytes 6148
  335.3 9.4 %copy-start.6 = (s32[64,8]{0,1:T(8,128)S(1)}, s32[64,8]{0,1:T(8,128)}, u32[]{:S(2)}) copy-start(s32[64,8]{0,1:T(8,128)} %param.17) | copy-start | bytes 6148
  335.3 10.7 %copy-start.9 = (s32[64]{0:T(128)S(1)}, s32[64]{0:T(128)}, u32[]{:S(2)}) copy-start(s32[64]{0:T(128)} %param.18) | copy-start | bytes 772
  336.4 28.9 %all-to-all-start = ((bf16[32,64,256]{2,1,0:T(8,128)(2,1)}), bf16[32,64,256]{2,1,0:T(8,128)(2,1)S(1)}, u32[]{:S(2)}, u32[]{:S(2)}) async-start(bf16[32,64,256]{2,1,0:T(8,128)(2,1)} %stack.2), calls=%async_computation.1 | async-start | bytes 2097152 | tf_op jit(solution)/shard_map/all_to_all | solution.py:12
  344.5 285.7 %reduce-scatter.5.cloned.1.call-start = ((), (), s32[]{:S(2)}) async-start(), calls=%async_computation.4 | async-start | bytes 1081344 | tf_op jit(solution)/shard_map/reduce_scatter | solution.py:90
  367.9 7.2 collective-permute-start
  376.3 13.0 %copy-start.1 = (bf16[2560,256]{1,0:T(8,128)(2,1)S(1)}, bf16[2560,256]{1,0:T(8,128)(2,1)}, u32[]{:S(2)}) copy-start(bf16[2560,256]{1,0:T(8,128)(2,1)} %pad_maximum_fusion) | copy-start | bytes 3932164
  378.5 16.1 %copy-start.5 = (bf16[64,256]{1,0:T(8,128)(2,1)S(1)}, bf16[64,256]{1,0:T(8,128)(2,1)}, u32[]{:S(2)}) copy-start(bf16[64,256]{1,0:T(8,128)(2,1)} %param.21) | copy-start | bytes 98308
  402.4 3.9 collective-permute-start.1
  412.3 217.8 %copy-start.2 = (f32[64,256]{1,0:T(8,128)S(1)}, f32[64,256]{1,0:T(8,128)}, u32[]{:S(2)}) copy-start(f32[64,256]{1,0:T(8,128)} %reduce-scatter.3.cloned.1.call-done) | copy-start | bytes 196612
  412.3 217.8 %copy-start.8 = (f32[256]{0:T(256)S(1)}, f32[256]{0:T(256)}, u32[]{:S(2)}) copy-start(f32[256]{0:T(256)} %param.15) | copy-start | bytes 3076
  415.0 292.7 %all-gather.2.cloned.1.call-start = ((), (), s32[]{:S(2)}) async-start(), calls=%async_computation.5 | async-start | bytes 1081344 | tf_op jit(solution)/shard_map/all_gather | solution.py:96
  631.6 78.7 %copy-start.11 = (bf16[1024,256]{1,0:T(8,128)(2,1)S(1)}, bf16[1024,256]{1,0:T(8,128)(2,1)}, u32[]{:S(2)}) copy-start(bf16[1024,256]{1,0:T(8,128)(2,1)} %param.20) | copy-start | bytes 1572868
  631.6 143.1 %all-reduce.2.cloned.1.call-start = ((), (), s32[]{:S(2)}) async-start(), calls=%async_computation.6 | async-start | bytes 655360 | tf_op jit(solution)/shard_map/psum | solution.py:100
Sparse Core Ops, SparseCore 0:
  113.7 220.6 reduce-scatter.2
  415.2 214.9 reduce-scatter.4
  633.3 74.3 all-gather.1
  710.4 64.2 all-reduce.1
